TPU v7x, 32 devices: a whole 2x2x4 slice. The times are simulated.
32 devices in a mesh: dp: 8 (over y, x, core), tensor: 4 (over z).
Axes of the slice: x: 2, y: 2, z: 4, core: 2. Of those that a mesh axis runs over, the one named last changes fastest.
Arguments:
- tokens: bfloat16 [1024, 8192], P('dp'), may hold values from -6 to 6
- target: bfloat16 [1024, 8192], P('dp'), may hold values from -6 to 6
- weight_in: bfloat16 [8192, 16384], P('dp', 'tensor'), may hold values from -0.125 to 0.125
- weight_out: bfloat16 [16384, 8192], P('tensor', 'dp'), may hold values from -0.09375 to 0.09375
- pattern: int32 [64, 128], replicated, may hold values from 0 to 1, as said below
Outputs:
- output: bfloat16 [1024, 8192], P('dp', 'tensor')
- hidden_target: bfloat16 [1024, 16384], P('dp', 'tensor')
Inputs may be any that keep to these rules, and one draw needn't show every extreme that they name: `pattern`: every entry is 0 or 1. A tile is the 8 row blocks of one index of dp with the 32 hidden blocks of one index of tensor; no tile holds more than 64 ones, and in every draw all tiles of one index of tensor hold exactly 64.
All inputs are finite; a program needn't handle non-finite values.
Results may differ from a plain program's by a relative error of at most 0.013.
Values may be sent and summed in bfloat16 or wider, within the bound.
A program may use at most 128 MiB of HBM per device.

v0:
```python
import jax
import jax.numpy as jnp
from jax import lax
from jax.sharding import PartitionSpec as P

BLK = 128


def slot_layout(pattern, column_start, blocks_down, blocks_across, peer_count, capacity):
    strip = lax.dynamic_slice_in_dim(pattern, column_start, blocks_across, 1)
    tile_size = blocks_down * blocks_across
    flat_mask = strip.reshape(peer_count, tile_size)
    position = jnp.cumsum(flat_mask, axis=1) - 1
    wanted = jnp.arange(capacity, dtype=jnp.int32)
    chosen = (
        (flat_mask[:, None, :] == 1) & (position[:, None, :] == wanted[None, :, None])
    ).astype(jnp.int32)
    within = jnp.sum(chosen * jnp.arange(tile_size, dtype=jnp.int32)[None, None, :], axis=2)
    return (chosen, within)


def one_hot_rows(index, count, dtype):
    return (index[:, None] == jnp.arange(count, dtype=jnp.int32)[None, :]).astype(dtype)


def spread_blocks(running, sources, weights, row_index, hidden_index, formula):
    row_hot = one_hot_rows(row_index, sources.shape[1], sources.dtype)
    picked = jnp.einsum("trb,sr->tsb", sources, row_hot, preferred_element_type=jnp.float32).astype(
        sources.dtype
    )
    product = jnp.einsum(formula, picked, weights, preferred_element_type=jnp.float32)
    hidden_hot = one_hot_rows(hidden_index, running.shape[1], jnp.float32)
    placed = jnp.einsum(
        "tsc,sj->tjc",
        product,
        hidden_hot,
        precision=lax.Precision.HIGHEST,
        preferred_element_type=jnp.float32,
    )
    return running + placed


def sweep_slots(running, sources, weights, row_index, hidden_index, formula, slot_step):
    slot_count = weights.shape[0]

    def advance(turn_index, carry):
        offset = turn_index * slot_step
        return spread_blocks(
            carry,
            sources,
            lax.dynamic_slice_in_dim(weights, offset, slot_step),
            lax.dynamic_slice_in_dim(row_index, offset, slot_step),
            lax.dynamic_slice_in_dim(hidden_index, offset, slot_step),
            formula,
        )

    return lax.fori_loop(0, slot_count // slot_step, advance, running)


def shards(tokens, target, weight_in, weight_out, pattern):
    peer_count = lax.axis_size("dp")
    data_rank = lax.axis_index("dp")
    tensor_rank = lax.axis_index("tensor")
    blocks_down = weight_in.shape[0] // BLK
    blocks_across = weight_in.shape[1] // BLK
    tile_size = blocks_down * blocks_across
    capacity = max(2, tile_size // 4)
    tok_rows = tokens.shape[0]
    all_rows = tokens.shape[1] // BLK
    chosen, within = slot_layout(
        pattern, tensor_rank * blocks_across, blocks_down, blocks_across, peer_count, capacity
    )
    own_pick = lax.dynamic_index_in_dim(chosen, data_rank, 0, keepdims=False).astype(jnp.bfloat16)
    in_tile = (
        weight_in.reshape(blocks_down, BLK, blocks_across, BLK)
        .transpose(0, 2, 1, 3)
        .reshape(tile_size, BLK, BLK)
    )
    out_tile = (
        weight_out.reshape(blocks_across, BLK, blocks_down, BLK)
        .transpose(2, 0, 1, 3)
        .reshape(tile_size, BLK, BLK)
    )
    packed_in = jnp.einsum(
        "cb,bxy->cxy", own_pick, in_tile, preferred_element_type=jnp.float32
    ).astype(jnp.bfloat16)
    packed_out = jnp.einsum(
        "cb,bxy->cxy", own_pick, out_tile, preferred_element_type=jnp.float32
    ).astype(jnp.bfloat16)
    local_row = within // blocks_across
    slot_hidden = (within % blocks_across).reshape(-1)
    slot_row = (local_row + jnp.arange(peer_count, dtype=jnp.int32)[:, None] * blocks_down).reshape(
        -1
    )
    group_peers = 1
    while group_peers * 2 * capacity <= 64 and peer_count % (group_peers * 2) == 0:
        group_peers = group_peers * 2
    slot_step = group_peers * capacity
    group_count = peer_count // group_peers
    token_blocks = tokens.reshape(tok_rows, all_rows, BLK)
    empty = jnp.zeros((tok_rows, blocks_across, BLK), jnp.float32)
    gathered_in, gathered_out = (
        lax.all_gather(packed_in, "dp", axis=0, tiled=True),
        lax.all_gather(packed_out, "dp", axis=0, tiled=True),
    )
    hidden = sweep_slots(
        empty, token_blocks, gathered_in, slot_row, slot_hidden, "tsb,sbc->tsc", slot_step
    )
    active = jnp.tanh(hidden).astype(jnp.bfloat16)
    place_count = group_peers * blocks_down
    peer_offset = jnp.arange(group_peers, dtype=jnp.int32)[:, None] * blocks_down

    def emit_rows(group_args):
        weights, hidden_index, row_index = group_args
        hidden_hot = one_hot_rows(hidden_index, blocks_across, jnp.bfloat16)
        picked = jnp.einsum(
            "tjh,sj->tsh", active, hidden_hot, preferred_element_type=jnp.float32
        ).astype(jnp.bfloat16)
        product = jnp.einsum("tsh,shd->tsd", picked, weights, preferred_element_type=jnp.float32)
        place_index = (row_index + peer_offset).reshape(-1)
        place_hot = one_hot_rows(place_index, place_count, jnp.float32)
        return jnp.einsum(
            "tsd,sq->tqd",
            product,
            place_hot,
            precision=lax.Precision.HIGHEST,
            preferred_element_type=jnp.float32,
        )

    pieces = lax.map(
        emit_rows,
        (
            gathered_out.reshape(group_count, slot_step, BLK, BLK),
            slot_hidden.reshape(group_count, slot_step),
            local_row.reshape(group_count, group_peers, capacity),
        ),
    )
    partial_value = pieces.transpose(1, 0, 2, 3).reshape(tok_rows, -1).astype(jnp.bfloat16)
    summed = lax.psum(partial_value, "tensor").astype(jnp.float32)
    whole_out = summed.astype(jnp.bfloat16)
    share_width = whole_out.shape[1] // lax.axis_size("tensor")
    output = lax.dynamic_slice_in_dim(whole_out, tensor_rank * share_width, share_width, 1)
    stacked = jnp.concatenate([whole_out, target], axis=0).reshape(2 * tok_rows, all_rows, BLK)
    zero_image = jnp.zeros((2 * tok_rows, blocks_across, BLK), jnp.float32)
    image = sweep_slots(
        zero_image, stacked, gathered_out, slot_row, slot_hidden, "tsd,shd->tsh", slot_step
    )
    feedback = jnp.tanh(image)
    hidden_target = active.astype(jnp.float32) + feedback[tok_rows:] - feedback[:tok_rows]
    return (output, hidden_target.reshape(tok_rows, -1).astype(jnp.bfloat16))


def solution(mesh):
    in_specs = (P("dp", None), P("dp", None), P("dp", "tensor"), P("tensor", "dp"), P())
    out_specs = (P("dp", "tensor"), P("dp", "tensor"))
    return jax.shard_map(shards, mesh=mesh, in_specs=in_specs, out_specs=out_specs, check_vma=False)
```

profile of v0, /device:TPU:0, one launch (start us, length us, event | category | flops | bytes accessed | tf_op | source)
XLA Modules:
  0.0 778.1 jit_solution(2342957863478818360)
XLA Ops:
  9.2 9.4 %copy.32 = bf16[128,8,32,128]{3,2,1,0:T(8,128)(2,1)} copy(bf16[128,8,32,128]{3,1,2,0:T(8,128)(2,1)} %bitcast.174) | data formatting | bytes 16777216
  26.6 9.2 %copy.16 = bf16[8,32,128,128]{3,1,0,2:T(8,128)(2,1)} copy(bf16[8,32,128,128]{3,1,2,0:T(8,128)(2,1)} %bitcast_bitcast_fusion) | data formatting | bytes 16777216 | tf_op jit(solution)/shard_map/transpose | solution.py:76
  42.5 8.8 %copy.31 = bf16[512,8,8,128]{3,2,1,0:T(8,128)(2,1)} copy(bf16[512,8,8,128]{3,1,2,0:T(8,128)(2,1)} %bitcast.175) | data formatting | bytes 16777216
  51.3 8.7 %bitcast_bitcast_fusion.1 = bf16[8,32,128,128]{3,0,2,1:T(8,128)(2,1)} fusion(bf16[32,128,8,128]{3,2,1,0:T(8,128)(2,1)} %bitcast.171), kind=kLoop, calls=%fused_computation.51 | loop fusion | bytes 16777216 | tf_op jit(solution)/shard_map/transpose | solution.py:81
  60.0 16.5 %copy.15 = bf16[8,32,128,128]{3,1,0,2:T(8,128)(2,1)} copy(bf16[8,32,128,128]{3,0,2,1:T(8,128)(2,1)} %bitcast_bitcast_fusion.1) | data formatting | bytes 16777216 | tf_op jit(solution)/shard_map/transpose | solution.py:81
  87.0 47.9 %all-gather.5.cloned.1.call-done = bf16[512,128,128]{2,0,1:T(8,128)(2,1)} async-done(((bf16[64,128,128]{2,0,1:T(8,128)(2,1)}), bf16[512,128,128]{2,0,1:T(8,128)(2,1)}) %all-gather.5.cloned.1.call-update) | async-done | bytes 16777232 | tf_op jit(solution)/shard_map/all_gather | solution.py:103
  134.9 148.5 %while.39 = (s32[]{:T(128)}, f32[128,32,128]{2,1,0:T(8,128)S(1)}, s32[512]{0:T(512)S(1)}, bf16[512,128,128]{2,0,1:T(8,128)(2,1)}, s32[512]{0:T(512)S(1)}, /*inde...) while((s32[]{:T(128)}, f32[128,32,128]{2,1,0:T(8,128)S(1)}, ...), condition=%wide.region_4.5_spmd.clone, body=%wide.region_3.4_spmd.clone.sunk | while | flops 806361088 | bytes 41944780 | solution.py:57
  283.7 137.6 %while.38 = (s32[]{:T(128)}, bf16[8,128,8,128]{3,2,1,0:T(8,128)(2,1)}, s32[8,1,64]{2,1,0:T(1,128)S(1)}, bf16[8,64,128,128]{3,1,0,2:T(8,128)(2,1)}, s32[8,64]{1,0...) while((s32[]{:T(128)}, bf16[8,128,8,128]{3,2,1,0:T(8,128)(2,1)}, s32[8,1,64]{2,1,0:T(1,128)S(1)}, ...), condition=%wide.region_6.7_spmd, body=%wide.region_5.6_spmd.sunk | while | flops 436210176 | bytes 28837476 | solution.py:130
  426.7 87.6 %all-reduce.2.cloned.1.call-done = bf16[128,8192]{1,0:T(8,128)(2,1)} async-done(((bf16[128,8192]{1,0:T(8,128)(2,1)}), bf16[128,8192]{1,0:T(8,128)(2,1)}) %all-reduce.2.cloned.1.call-update) | async-done | bytes 2097168 | tf_op jit(solution)/shard_map/psum | solution.py:139
  520.2 244.3 %while.40 = (s32[]{:T(128)}, f32[256,32,128]{2,1,0:T(8,128)}, s32[512]{0:T(512)S(1)}, bf16[512,128,128]{2,0,1:T(8,128)(2,1)}, s32[512]{0:T(512)S(1)}, /*index=5*...) while((s32[]{:T(128)}, f32[256,32,128]{2,1,0:T(8,128)}, ...), condition=%wide.region_9.10_spmd.clone, body=%wide.region_8.9_spmd.clone.sunk | while | flops 1612716032 | bytes 77596360 | solution.py:57
  532.5 8.7 %copy.76 = f32[64,128,256]{1,0,2:T(8,128)} copy(f32[64,128,256]{2,1,0:T(8,128)} %fusion.119) | data formatting | bytes 16777216 | tf_op jit(solution)/shard_map/while/body/eval_jaxpr/tsd,shd->tsh/dot_general | solution.py:31
  561.9 8.7 %copy.76 = f32[64,128,256]{1,0,2:T(8,128)} copy(f32[64,128,256]{2,1,0:T(8,128)} %fusion.119) | data formatting | bytes 16777216 | tf_op jit(solution)/shard_map/while/body/eval_jaxpr/tsd,shd->tsh/dot_general | solution.py:31
  570.7 9.8 %bitcast_add_fusion.5 = f32[256,32,128]{2,1,0:T(8,128)} fusion(f32[256,32,128]{2,1,0:T(8,128)} %get-tuple-element.546, f32[64,128,256]{1,0,2:T(8,128)} %copy.76, pred[]{:T(512)S(6)} %compare.21, s32[64]{0:T(128)S(1)} %dynamic_slice.108), kind=kOutput, calls=%fused_computation.40.clone.1 | convolution fusion | flops 807405568 | bytes 16777472 | tf_op jit(solution)/shard_map/while/body/eval_jaxpr/tsc,sj->tjc/dot_general | solution.py:33
  592.6 8.7 %copy.76 = f32[64,128,256]{1,0,2:T(8,128)} copy(f32[64,128,256]{2,1,0:T(8,128)} %fusion.119) | data formatting | bytes 16777216 | tf_op jit(solution)/shard_map/while/body/eval_jaxpr/tsd,shd->tsh/dot_general | solution.py:31
  601.3 9.8 %bitcast_add_fusion.5 = f32[256,32,128]{2,1,0:T(8,128)} fusion(f32[256,32,128]{2,1,0:T(8,128)} %get-tuple-element.546, f32[64,128,256]{1,0,2:T(8,128)} %copy.76, pred[]{:T(512)S(6)} %compare.21, s32[64]{0:T(128)S(1)} %dynamic_slice.108), kind=kOutput, calls=%fused_computation.40.clone.1 | convolution fusion | flops 807405568 | bytes 16777472 | tf_op jit(solution)/shard_map/while/body/eval_jaxpr/tsc,sj->tjc/dot_general | solution.py:33
  623.3 8.7 %copy.76 = f32[64,128,256]{1,0,2:T(8,128)} copy(f32[64,128,256]{2,1,0:T(8,128)} %fusion.119) | data formatting | bytes 16777216 | tf_op jit(solution)/shard_map/while/body/eval_jaxpr/tsd,shd->tsh/dot_general | solution.py:31
  632.0 9.8 %bitcast_add_fusion.5 = f32[256,32,128]{2,1,0:T(8,128)} fusion(f32[256,32,128]{2,1,0:T(8,128)} %get-tuple-element.546, f32[64,128,256]{1,0,2:T(8,128)} %copy.76, pred[]{:T(512)S(6)} %compare.21, s32[64]{0:T(128)S(1)} %dynamic_slice.108), kind=kOutput, calls=%fused_computation.40.clone.1 | convolution fusion | flops 807405568 | bytes 16777472 | tf_op jit(solution)/shard_map/while/body/eval_jaxpr/tsc,sj->tjc/dot_general | solution.py:33
  654.0 8.7 %copy.76 = f32[64,128,256]{1,0,2:T(8,128)} copy(f32[64,128,256]{2,1,0:T(8,128)} %fusion.119) | data formatting | bytes 16777216 | tf_op jit(solution)/shard_map/while/body/eval_jaxpr/tsd,shd->tsh/dot_general | solution.py:31
  662.7 9.8 %bitcast_add_fusion.5 = f32[256,32,128]{2,1,0:T(8,128)} fusion(f32[256,32,128]{2,1,0:T(8,128)} %get-tuple-element.546, f32[64,128,256]{1,0,2:T(8,128)} %copy.76, pred[]{:T(512)S(6)} %compare.21, s32[64]{0:T(128)S(1)} %dynamic_slice.108), kind=kOutput, calls=%fused_computation.40.clone.1 | convolution fusion | flops 807405568 | bytes 16777472 | tf_op jit(solution)/shard_map/while/body/eval_jaxpr/tsc,sj->tjc/dot_general | solution.py:33
  684.6 8.7 %copy.76 = f32[64,128,256]{1,0,2:T(8,128)} copy(f32[64,128,256]{2,1,0:T(8,128)} %fusion.119) | data formatting | bytes 16777216 | tf_op jit(solution)/shard_map/while/body/eval_jaxpr/tsd,shd->tsh/dot_general | solution.py:31
  693.4 9.8 %bitcast_add_fusion.5 = f32[256,32,128]{2,1,0:T(8,128)} fusion(f32[256,32,128]{2,1,0:T(8,128)} %get-tuple-element.546, f32[64,128,256]{1,0,2:T(8,128)} %copy.76, pred[]{:T(512)S(6)} %compare.21, s32[64]{0:T(128)S(1)} %dynamic_slice.108), kind=kOutput, calls=%fused_computation.40.clone.1 | convolution fusion | flops 807405568 | bytes 16777472 | tf_op jit(solution)/shard_map/while/body/eval_jaxpr/tsc,sj->tjc/dot_general | solution.py:33
  715.3 8.7 %copy.76 = f32[64,128,256]{1,0,2:T(8,128)} copy(f32[64,128,256]{2,1,0:T(8,128)} %fusion.119) | data formatting | bytes 16777216 | tf_op jit(solution)/shard_map/while/body/eval_jaxpr/tsd,shd->tsh/dot_general | solution.py:31
  724.0 9.8 %bitcast_add_fusion.5 = f32[256,32,128]{2,1,0:T(8,128)} fusion(f32[256,32,128]{2,1,0:T(8,128)} %get-tuple-element.546, f32[64,128,256]{1,0,2:T(8,128)} %copy.76, pred[]{:T(512)S(6)} %compare.21, s32[64]{0:T(128)S(1)} %dynamic_slice.108), kind=kOutput, calls=%fused_computation.40.clone.1 | convolution fusion | flops 807405568 | bytes 16777472 | tf_op jit(solution)/shard_map/while/body/eval_jaxpr/tsc,sj->tjc/dot_general | solution.py:33
  754.7 9.8 %bitcast_add_fusion.5 = f32[256,32,128]{2,1,0:T(8,128)} fusion(f32[256,32,128]{2,1,0:T(8,128)} %get-tuple-element.546, f32[64,128,256]{1,0,2:T(8,128)} %copy.76, pred[]{:T(512)S(6)} %compare.21, s32[64]{0:T(128)S(1)} %dynamic_slice.108), kind=kOutput, calls=%fused_computation.40.clone.1 | convolution fusion | flops 807405568 | bytes 16777472 | tf_op jit(solution)/shard_map/while/body/eval_jaxpr/tsc,sj->tjc/dot_general | solution.py:33
  (227 shorter events, 444.6 us)
Async XLA Ops:
  7.2 127.7 %all-gather.5.cloned.1.call-start = ((), (), s32[]{:S(2)}) async-start(), calls=%async_computation.1 | async-start | bytes 18874368 | tf_op jit(solution)/shard_map/all_gather | solution.py:103
  42.3 241.4 %all-gather.3.cloned.1.call-start = ((), (), s32[]{:S(2)}) async-start(), calls=%async_computation | async-start | bytes 18874368 | tf_op jit(solution)/shard_map/all_gather | solution.py:104
  82.8 431.5 %all-reduce.2.cloned.1.call-start = ((), (), s32[]{:S(2)}) async-start(), calls=%async_computation.2 | async-start | bytes 4194304 | tf_op jit(solution)/shard_map/psum | solution.py:139
  135.0 2.2 copy-start.1
  154.0 2.2 copy-start.1
  172.4 2.2 copy-start.1
  190.9 2.5 copy-start.1
  209.7 2.2 copy-start.1
  228.1 2.2 copy-start.1
  246.6 2.2 copy-start.1
  265.1 2.2 copy-start.1
  520.5 2.8 copy-start
  550.0 2.8 copy-start
  580.7 2.8 copy-start
  611.3 2.8 copy-start
  642.0 2.8 copy-start
  672.7 2.8 copy-start
  703.3 2.8 copy-start
  734.0 2.8 copy-start
Sparse Core Ops, SparseCore 0:
  42.4 92.4 all-gather.4
  136.8 89.7 all-gather.2
  426.8 87.4 all-reduce.1
where the time goes:
time: 786 us; the launch traced here: 778 us
  matrix products  328 us (42%)
  local copies, waits for them, and re-layouts  294 us (37%)
  waiting for transfers between devices  136 us (17%)
  between operations  14.1 us (2%)
    dot_general x16, matrix products, spread_blocks(): jnp.einsum('tsc,sj->tjc', product, hidden_hot, precision=lax.Precision.HI...  117 us
    dot_general x16, local copies, waits for them, and re-layouts, spread_blocks(): jnp.einsum(formula, picked, weights, preferred_element_type=jnp.float32)  114 us
    dot_general x16, matrix products, spread_blocks(): jnp.einsum(formula, picked, weights, preferred_element_type=jnp.float32)  102 us
    psum x1, waiting for transfers between devices, shards(): summed = lax.psum(partial_value, 'tensor').astype(jnp.float32)  87.6 us
    all_gather x1, waiting for transfers between devices, shards(): lax.all_gather(packed_in, 'dp', axis=0, tiled=True)  47.9 us
    dot_general x8, local copies, waits for them, and re-layouts, emit_rows(): jnp.einsum('tsh,shd->tsd', picked, weights, preferred_element_type=jnp.fl...  43.2 us
    dot_general x8, matrix products, emit_rows(): jnp.einsum('tsh,shd->tsd', picked, weights, preferred_element_type=jnp.fl...  38.8 us
    dot_general x8, matrix products, emit_rows(): jnp.einsum('tsd,sq->tqd', product, place_hot, precision=lax.Precision.HIG...  34.8 us
  transfers between devices with their start and end apart: 3, of which 2 were waited for; matrix products, arithmetic and copies ran while one was open for 24% of the time, Pallas kernels for 0%

commit v1 on v0

--- a/solution.py
+++ b/solution.py
@@ -136,7 +136,7 @@
         ),
     )
     partial_value = pieces.transpose(1, 0, 2, 3).reshape(tok_rows, -1).astype(jnp.bfloat16)
-    summed = lax.psum(partial_value, "tensor").astype(jnp.float32)
+    summed = jnp.sum(lax.all_gather(partial_value, "tensor"), axis=0).astype(jnp.float32)
     whole_out = summed.astype(jnp.bfloat16)
     share_width = whole_out.shape[1] // lax.axis_size("tensor")
     output = lax.dynamic_slice_in_dim(whole_out, tensor_rank * share_width, share_width, 1)

time: 786 us -> 910 us (1.16)
  waiting for transfers between devices: 136 us -> 196 us
  local copies, waits for them, and re-layouts: 294 us -> 330 us
  matrix products: 328 us -> 346 us
    dot_general x24 -> x0, local copies, waits for them, and re-layouts: 157 us -> none  [the longest x16 114 us: spread_blocks(): jnp.einsum(formula, picked, weights, preferred_element_type=jnp.float32)]
    transpose x0 -> x24, local copies, waits for them, and re-layouts: none -> 157 us  [the longest x16 113 us: spread_blocks(): jnp.einsum(formula, picked, weights, preferred_element_type=jnp.float32)]
    all_gather x0 -> x1, waiting for transfers between devices: none -> 148 us  [shards(): lax.all_gather(partial_value, 'tensor')]
    psum x1 -> x0, waiting for transfers between devices: 87.6 us -> none  [shards(): summed = lax.psum(partial_value, 'tensor').astype(jnp.float32)]
    dynamic_slice x8 -> x16, local copies, waits for them, and re-layouts: 14.3 us -> 37.5 us  [shards(): lax.map(emit_rows, (gathered_out.reshape(group_count, slot_step, BLK, BLK...]
    dot_general x8, matrix products: 38.8 us -> 51.5 us  [emit_rows(): jnp.einsum('tsh,shd->tsd', picked, weights, preferred_element_type=jnp.fl...]
    dot_general x8, matrix products: 5.96 us -> 16.6 us  [emit_rows(): jnp.einsum('tjh,sj->tsh', active, hidden_hot, preferred_element_type=jnp....]
    unnamed x6 -> x14, local copies, waits for them, and re-layouts: 29.6 us -> 37.5 us
  transfers between devices with their start and end apart: 3 -> 3, of which waited for: 2 -> 2; matrix products, arithmetic and copies ran while one was open for 24% -> 21% of each run, Pallas kernels for 0% -> 0%
where the time goes in v1:
time: 910 us; the launch traced here: 902 us
  matrix products  346 us (38%)
  local copies, waits for them, and re-layouts  330 us (36%)
  waiting for transfers between devices  196 us (22%)
  between operations  14.1 us (2%)
  other arithmetic  13.8 us (2%)
    all_gather x1, waiting for transfers between devices, shards(): lax.all_gather(partial_value, 'tensor')  148 us
    dot_general x16, matrix products, spread_blocks(): jnp.einsum('tsc,sj->tjc', product, hidden_hot, precision=lax.Precision.HI...  117 us
    transpose x16, local copies, waits for them, and re-layouts, spread_blocks(): jnp.einsum(formula, picked, weights, preferred_element_type=jnp.float32)  113 us
    dot_general x16, matrix products, spread_blocks(): jnp.einsum(formula, picked, weights, preferred_element_type=jnp.float32)  103 us
    dot_general x8, matrix products, emit_rows(): jnp.einsum('tsh,shd->tsd', picked, weights, preferred_element_type=jnp.fl...  51.5 us
    all_gather x1, waiting for transfers between devices, shards(): lax.all_gather(packed_in, 'dp', axis=0, tiled=True)  48 us
    transpose x8, local copies, waits for them, and re-layouts, emit_rows(): jnp.einsum('tsh,shd->tsd', picked, weights, preferred_element_type=jnp.fl...  43.2 us
    unnamed x14, local copies, waits for them, and re-layouts  37.5 us
  transfers between devices with their start and end apart: 3, of which 2 were waited for; matrix products, arithmetic and copies ran while one was open for 21% of the time, Pallas kernels for 0%

profile of v1, /device:TPU:0, one launch (start us, length us, event | category | flops | bytes accessed | tf_op | source)
XLA Modules:
  0.0 901.7 jit_solution(15657535730002929220)
XLA Ops:
  9.2 9.4 %copy.47 = bf16[128,8,32,128]{3,2,1,0:T(8,128)(2,1)} copy(bf16[128,8,32,128]{3,1,2,0:T(8,128)(2,1)} %bitcast.160) | data formatting | bytes 16777216
  26.6 9.3 %copy.29 = bf16[8,32,128,128]{3,1,0,2:T(8,128)(2,1)} copy(bf16[8,32,128,128]{3,1,2,0:T(8,128)(2,1)} %bitcast_bitcast_fusion) | data formatting | bytes 16777216 | tf_op jit(solution)/shard_map/transpose | solution.py:76
  42.5 8.8 copy.46
  51.3 8.7 bitcast_bitcast_fusion.1
  60.0 16.5 %copy.28 = bf16[8,32,128,128]{3,1,0,2:T(8,128)(2,1)} copy(bf16[8,32,128,128]{3,0,2,1:T(8,128)(2,1)} %bitcast_bitcast_fusion.1) | data formatting | bytes 16777216 | tf_op jit(solution)/shard_map/transpose | solution.py:81
  87.0 48.0 %all-gather.6.cloned.1.call-done = bf16[512,128,128]{2,0,1:T(8,128)(2,1)} async-done(((bf16[64,128,128]{2,0,1:T(8,128)(2,1)}), bf16[512,128,128]{2,0,1:T(8,128)(2,1)}) %all-gather.6.cloned.1.call-update) | async-done | bytes 16777232 | tf_op jit(solution)/shard_map/all_gather | solution.py:103
  134.9 147.7 %while.39 = (s32[]{:T(128)}, f32[128,32,128]{2,1,0:T(8,128)S(1)}, s32[512]{0:T(512)S(1)}, bf16[512,128,128]{2,0,1:T(8,128)(2,1)}, s32[512]{0:T(512)S(1)}, /*inde...) while((s32[]{:T(128)}, f32[128,32,128]{2,1,0:T(8,128)S(1)}, ...), condition=%wide.region_4.5_spmd.clone, body=%wide.region_3.4_spmd.clone.sunk | while | flops 807409664 | bytes 41944780 | solution.py:57
  284.0 186.1 %while.38 = (s32[]{:T(128)}, bf16[8,128,8,128]{1,3,2,0:T(8,128)(2,1)}, s32[8,1,64]{2,1,0:T(1,128)S(1)}, bf16[8,64,128,128]{3,1,0,2:T(8,128)(2,1)}, s32[8,64]{1,0...) while((s32[]{:T(128)}, bf16[8,128,8,128]{1,3,2,0:T(8,128)(2,1)}, s32[8,1,64]{2,1,0:T(1,128)S(1)}, ...), condition=%wide.region_6.7_spmd, body=%wide.region_5.6_spmd.sunk | while | flops 437258752 | bytes 33818212 | solution.py:130
  476.9 148.3 %all-gather.8.cloned.1.call-done = bf16[4,128,8192]{2,1,0:T(8,128)(2,1)} async-done(((bf16[1,128,8192]{2,1,0:T(8,128)(2,1)}), bf16[4,128,8192]{2,1,0:T(8,128)(2,1)}) %all-gather.8.cloned.1.call-update) | async-done | bytes 8388624 | tf_op jit(solution)/shard_map/all_gather | solution.py:139
  646.9 243.0 %while.40 = (s32[]{:T(128)}, f32[256,32,128]{2,1,0:T(8,128)}, s32[512]{0:T(512)S(1)}, bf16[512,128,128]{2,0,1:T(8,128)(2,1)}, s32[512]{0:T(512)S(1)}, /*index=5*...) while((s32[]{:T(128)}, f32[256,32,128]{2,1,0:T(8,128)}, ...), condition=%wide.region_9.10_spmd.clone, body=%wide.region_8.9_spmd.clone.sunk | while | flops 1614813184 | bytes 77596360 | solution.py:57
  659.0 8.7 copy.83
  688.3 8.7 copy.83
  697.0 9.8 %bitcast_add_fusion.5 = f32[256,32,128]{2,1,0:T(8,128)} fusion(f32[256,32,128]{2,1,0:T(8,128)} %get-tuple-element.566, f32[256,64,128]{2,1,0:T(8,128)} %copy.83, pred[]{:T(512)S(6)} %compare.21, s32[64]{0:T(128)S(1)} %dynamic_slice.108), kind=kOutput, calls=%fused_computation.29.clone.1 | convolution fusion | flops 807405568 | bytes 16777472 | tf_op jit(solution)/shard_map/while/body/eval_jaxpr/tsc,sj->tjc/dot_general | solution.py:33
  718.8 8.7 copy.83
  727.5 9.8 %bitcast_add_fusion.5 = f32[256,32,128]{2,1,0:T(8,128)} fusion(f32[256,32,128]{2,1,0:T(8,128)} %get-tuple-element.566, f32[256,64,128]{2,1,0:T(8,128)} %copy.83, pred[]{:T(512)S(6)} %compare.21, s32[64]{0:T(128)S(1)} %dynamic_slice.108), kind=kOutput, calls=%fused_computation.29.clone.1 | convolution fusion | flops 807405568 | bytes 16777472 | tf_op jit(solution)/shard_map/while/body/eval_jaxpr/tsc,sj->tjc/dot_general | solution.py:33
  749.3 8.7 copy.83
  758.0 9.8 %bitcast_add_fusion.5 = f32[256,32,128]{2,1,0:T(8,128)} fusion(f32[256,32,128]{2,1,0:T(8,128)} %get-tuple-element.566, f32[256,64,128]{2,1,0:T(8,128)} %copy.83, pred[]{:T(512)S(6)} %compare.21, s32[64]{0:T(128)S(1)} %dynamic_slice.108), kind=kOutput, calls=%fused_computation.29.clone.1 | convolution fusion | flops 807405568 | bytes 16777472 | tf_op jit(solution)/shard_map/while/body/eval_jaxpr/tsc,sj->tjc/dot_general | solution.py:33
  779.8 8.7 copy.83
  788.5 9.8 %bitcast_add_fusion.5 = f32[256,32,128]{2,1,0:T(8,128)} fusion(f32[256,32,128]{2,1,0:T(8,128)} %get-tuple-element.566, f32[256,64,128]{2,1,0:T(8,128)} %copy.83, pred[]{:T(512)S(6)} %compare.21, s32[64]{0:T(128)S(1)} %dynamic_slice.108), kind=kOutput, calls=%fused_computation.29.clone.1 | convolution fusion | flops 807405568 | bytes 16777472 | tf_op jit(solution)/shard_map/while/body/eval_jaxpr/tsc,sj->tjc/dot_general | solution.py:33
  819.0 9.8 %bitcast_add_fusion.5 = f32[256,32,128]{2,1,0:T(8,128)} fusion(f32[256,32,128]{2,1,0:T(8,128)} %get-tuple-element.566, f32[256,64,128]{2,1,0:T(8,128)} %copy.83, pred[]{:T(512)S(6)} %compare.21, s32[64]{0:T(128)S(1)} %dynamic_slice.108), kind=kOutput, calls=%fused_computation.29.clone.1 | convolution fusion | flops 807405568 | bytes 16777472 | tf_op jit(solution)/shard_map/while/body/eval_jaxpr/tsc,sj->tjc/dot_general | solution.py:33
  840.8 8.7 copy.83
  849.5 9.8 %bitcast_add_fusion.5 = f32[256,32,128]{2,1,0:T(8,128)} fusion(f32[256,32,128]{2,1,0:T(8,128)} %get-tuple-element.566, f32[256,64,128]{2,1,0:T(8,128)} %copy.83, pred[]{:T(512)S(6)} %compare.21, s32[64]{0:T(128)S(1)} %dynamic_slice.108), kind=kOutput, calls=%fused_computation.29.clone.1 | convolution fusion | flops 807405568 | bytes 16777472 | tf_op jit(solution)/shard_map/while/body/eval_jaxpr/tsc,sj->tjc/dot_general | solution.py:33
  871.3 8.7 copy.83
  880.0 9.8 %bitcast_add_fusion.5 = f32[256,32,128]{2,1,0:T(8,128)} fusion(f32[256,32,128]{2,1,0:T(8,128)} %get-tuple-element.566, f32[256,64,128]{2,1,0:T(8,128)} %copy.83, pred[]{:T(512)S(6)} %compare.21, s32[64]{0:T(128)S(1)} %dynamic_slice.108), kind=kOutput, calls=%fused_computation.29.clone.1 | convolution fusion | flops 807405568 | bytes 16777472 | tf_op jit(solution)/shard_map/while/body/eval_jaxpr/tsc,sj->tjc/dot_general | solution.py:33
  (260 shorter events, 507.4 us)
Async XLA Ops:
  7.2 127.8 %all-gather.6.cloned.1.call-start = ((), (), s32[]{:S(2)}) async-start(), calls=%async_computation.1 | async-start | bytes 18874368 | tf_op jit(solution)/shard_map/all_gather | solution.py:103
  42.3 240.7 %all-gather.4.cloned.1.call-start = ((), (), s32[]{:S(2)}) async-start(), calls=%async_computation | async-start | bytes 18874368 | tf_op jit(solution)/shard_map/all_gather | solution.py:104
  82.8 542.4 %all-gather.8.cloned.1.call-start = ((), (), s32[]{:S(2)}) async-start(), calls=%async_computation.2 | async-start | bytes 10485760 | tf_op jit(solution)/shard_map/all_gather | solution.py:139
  134.9 2.2 copy-start.3
  153.7 2.2 copy-start.3
  172.0 2.2 copy-start.3
  190.8 2.5 copy-start.3
  209.4 2.2 copy-start.3
  227.7 2.2 copy-start.3
  246.0 2.2 copy-start.3
  264.4 2.2 copy-start.3
  282.7 1.3 copy-start.1
  470.1 4.3 copy-start.4
  647.0 2.8 copy-start
  676.3 2.8 copy-start
  706.8 2.8 copy-start
  737.3 2.8 copy-start
  767.9 2.8 copy-start
  798.4 2.8 copy-start
  828.9 2.8 copy-start
  859.4 2.8 copy-start
  889.9 2.9 copy-start.2
Sparse Core Ops, SparseCore 0:
  42.4 92.4 all-gather.5
  136.8 89.6 all-gather.3
  474.5 150.6 all-gather.7
